TPU v7x, 128 devices: a whole 4x4x4 slice. The times are simulated.
128 devices in a mesh: dp: 16 (over y, z), ctx: 8 (over x, core).
Axes of the slice: x: 4, y: 4, z: 4, core: 2. Of those that a mesh axis runs over, the one named last changes fastest.
Arguments:
- input_entries: bfloat16 [16, 2048, 8192], P('dp', 'ctx'), may hold values from -6 to 6
- segment_entry_counts: int32 [16, 8, 8], P('dp'), may hold values from 1 to 64, as said below
- segment_destination_part: int32 [16, 8, 8], P('dp'), may hold values from 0 to 7, as said below
- norm_gain: float32 [8192], replicated, may hold values from 0.25 to 1.75
- kv_weight: bfloat16 [8192, 2048], P('dp'), may hold values from -0.0625 to 0.0625
- kv_bias: float32 [2048], replicated, may hold values from -3 to 3
Outputs:
- evened_residual_entries: bfloat16 [16, 2048, 8192], P('dp', 'ctx')
- lookup_stored_tensors: bfloat16 [16, 2048, 2, 8, 128], P('dp', None, None, 'ctx')
Inputs may be any that keep to these rules, and one draw needn't show every extreme that they name: `segment_entry_counts`: in each sequence the runs of one shard cover its 256 rows; every shard receives exactly 256 rows; at most 64 rows go from one shard to one shard, and every sequence has a run of exactly 64. The numbers of rows between shards form a Latin arrangement: every shard sends the same list of 8 numbers, one to each shard, and receives each number of that list once. `segment_destination_part`: the 8 runs of one shard go to 8 different shards.
All inputs are finite; a program needn't handle non-finite values.
Results may differ from a plain program's by a relative error of at most 0.0046.
Values may be sent and summed in bfloat16 or wider, within the bound.
A program may use at most 192 MiB of HBM per device.

v0:
```python
import jax
import jax.numpy as jnp
from jax import lax
from jax.sharding import PartitionSpec as P

KVH = 8
HD = 128


def plan_tables(lengths, targets, peer_count):
    labels = jnp.arange(peer_count, dtype=jnp.int32)
    starts = jnp.cumsum(lengths, axis=1) - lengths
    matches = (targets[:, :, None] == labels[None, None, :]).astype(jnp.int32)
    counts = jnp.sum(lengths[:, :, None] * matches, axis=1)
    anchors = jnp.sum(starts[:, :, None] * matches, axis=1)
    run_ends = jnp.cumsum(counts, axis=0)
    offsets = run_ends - counts
    return (counts, anchors, offsets, run_ends)


def source_of(positions, ends_column, offsets_column, anchors_column, peer_count):
    labels = jnp.arange(peer_count, dtype=jnp.int32)
    source = jnp.sum((ends_column[None, :] <= positions[:, None]).astype(jnp.int32), axis=1)
    chosen = (source[:, None] == labels[None, :]).astype(jnp.int32)
    within = positions - jnp.sum(chosen * offsets_column[None, :], axis=1)
    anchor = jnp.sum(chosen * anchors_column[None, :], axis=1)
    return (source, within, anchor)


def rms_normed(rows, norm_gain):
    as_float = rows.astype(jnp.float32)
    inverse_rms = lax.rsqrt(jnp.mean(as_float * as_float, axis=-1, keepdims=True) + 1e-06)
    return (as_float * inverse_rms * norm_gain[None, :]).astype(jnp.bfloat16)


def pack_document_runs(rows, counts, anchors, myself, peer_count):
    row_count = rows.shape[0]
    capacity = 2 * row_count // peer_count
    slot_index = jnp.arange(capacity, dtype=jnp.int32)
    my_counts = counts[myself]
    my_anchors = anchors[myself]
    wanted = jnp.minimum(my_anchors[:, None] + slot_index[None, :], row_count - 1)
    is_live = slot_index[None, :] < my_counts[:, None]
    picked = jnp.take(rows, wanted.reshape(-1), axis=0).reshape(peer_count, capacity, -1)
    return jnp.where(is_live[:, :, None], picked, jnp.zeros_like(picked))


def unpack_runs(arriving_rows, positions, run_ends, offsets, anchors, myself, peer_count):
    capacity = arriving_rows.shape[1]
    source, within, anchor = source_of(
        positions, run_ends[:, myself], offsets[:, myself], anchors[:, myself], peer_count
    )
    flat_rows = arriving_rows.reshape(peer_count * capacity, -1)
    return jnp.take(flat_rows, source * capacity + within, axis=0)


def on_device(
    input_entries, segment_entry_counts, segment_destination_part, norm_gain, kv_weight, kv_bias
):
    peer_count = lax.axis_size("ctx")
    myself = lax.axis_index("ctx")
    row_count = input_entries.shape[1]
    counts, anchors, offsets, run_ends = plan_tables(
        segment_entry_counts[0], segment_destination_part[0], peer_count
    )
    positions = jnp.arange(row_count, dtype=jnp.int32)
    outgoing = pack_document_runs(input_entries[0], counts, anchors, myself, peer_count)
    arriving_rows = lax.all_to_all(outgoing, "ctx", split_axis=0, concat_axis=0, tiled=True)
    moved_rows = unpack_runs(
        arriving_rows, positions, run_ends, offsets, anchors, myself, peer_count
    )
    normed = rms_normed(moved_rows, norm_gain)
    summed_squares = jnp.dot(
        normed,
        lax.all_gather(kv_weight, "dp", axis=0, tiled=True),
        preferred_element_type=jnp.float32,
    )
    mapped_outputs = (
        (summed_squares + kv_bias[None, :]).astype(jnp.bfloat16).reshape(1, row_count, 2, KVH, HD)
    )
    by_heads = lax.all_to_all(mapped_outputs, "ctx", split_axis=3, concat_axis=1, tiled=True)
    return (moved_rows[None], by_heads)


def solution(mesh):
    in_specs = (
        P("dp", "ctx", None),
        P("dp", None, None),
        P("dp", None, None),
        P(),
        P("dp", None),
        P(),
    )
    out_specs = (P("dp", "ctx", None), P("dp", None, None, "ctx", None))
    return jax.shard_map(
        on_device, mesh=mesh, in_specs=in_specs, out_specs=out_specs, check_vma=False
    )
```

profile of v0, /device:TPU:1, one launch (start us, length us, event | category | flops | bytes accessed | tf_op | source)
XLA Modules:
  0.0 256.8 jit_solution(8461394061242989045)
XLA Ops:
  7.2 0.0 all-gather.2.cloned.1.call-start
  7.2 0.7 all-gather.2.cloned.1.call-update
  7.9 0.8 reduce_window_sum.23
  8.7 0.7 bitcast_subtract_fusion
  9.4 0.8 select_reduce_fusion.1
  10.3 0.1 add_minimum_fusion
  10.3 0.1 min.22
  10.4 18.2 %gather_fusion = bf16[512,8192]{1,0:T(8,128)(2,1)} fusion(bf16[256,8192]{1,0:T(8,128)(2,1)} %bitcast.28, s32[1024]{0:T(1024)S(1)} %pad_clamp_fusion.1), kind=kCustom, calls=%fused_computation | custom fusion | bytes 16779264 | tf_op jit(solution)/shard_map/jit(_take)/gather | solution.py:44
  28.6 0.1 compare_and_fusion
  28.7 0.1 iota_compare_fusion.3
  28.8 7.6 %select_select_fusion = bf16[8,64,8192]{2,1,0:T(8,128)(2,1)} fusion(bf16[8,64,8192]{2,1,0:T(8,128)(2,1)} %bitcast.29, pred[8,64]{1,0:T(8,128)(4,1)S(1)} %compare_and_fusion, pred[8,64]{1,0:T(8,128)(4,1)S(1)} %iota_compare_fusion.3), kind=kLoop, calls=%fused_computation.7 | loop fusion | flops 8388608 | bytes 16778240 | tf_op jit(solution)/shard_map/jit(_where)/select_n | solution.py:45
  36.4 6.3 %all-to-all-start = ((bf16[8,64,8192]{2,1,0:T(8,128)(2,1)}), bf16[8,64,8192]{2,1,0:T(8,128)(2,1)}, u32[]{:S(2)}, u32[]{:S(2)}) async-start(bf16[8,64,8192]{2,1,0:T(8,128)(2,1)} %select_select_fusion), calls=%async_computation | async-start | bytes 16777216 | tf_op jit(solution)/shard_map/all_to_all | solution.py:68
  42.7 0.2 dynamic-slice_reduce_fusion
  42.9 0.1 convert_reduce_fusion
  43.0 0.1 select_reduce_fusion.2
  43.1 93.4 %all-to-all-done = bf16[8,64,8192]{2,1,0:T(8,128)(2,1)} async-done(((bf16[8,64,8192]{2,1,0:T(8,128)(2,1)}), bf16[8,64,8192]{2,1,0:T(8,128)(2,1)}, u32[]{:S(2)}, u32[]{:S(2)}) %all-to-all-start) | async-done | bytes 8388640 | tf_op jit(solution)/shard_map/all_to_all | solution.py:68
  136.5 13.6 %gather_fusion.1 = bf16[256,8192]{1,0:T(8,128)(2,1)} fusion(bf16[512,8192]{1,0:T(8,128)(2,1)} %bitcast.7, s32[1024]{0:T(1024)S(1)} %pad_clamp_fusion), kind=kCustom, calls=%fused_computation.1 | custom fusion | bytes 8389632 | tf_op jit(solution)/shard_map/jit(_take)/gather | solution.py:54
  150.1 0.0 copy-start
  150.1 0.0 copy-start.1
  150.1 3.4 %fusion = f32[256]{0:T(256)S(1)} fusion(bf16[256,8192]{1,0:T(8,128)(2,1)} %gather_fusion.1, pred[256]{0:T(512)(128)(4,1)S(1)} %compare_and_fusion.1), kind=kLoop, calls=%fused_computation.4 | loop fusion | flops 8388352 | bytes 4195584 | tf_op jit(solution)/shard_map/reduce_sum | solution.py:32
  153.6 57.0 %all-gather.2.cloned.1.call-done = bf16[8192,2048]{1,0:T(8,128)(2,1)} async-done(((bf16[512,2048]{1,0:T(8,128)(2,1)}), bf16[8192,2048]{1,0:T(8,128)(2,1)}) %all-gather.2.cloned.1.call-update) | async-done | bytes 33554448 | tf_op jit(solution)/shard_map/all_gather | solution.py:75
  210.6 0.0 copy-done
  210.6 0.0 copy-done.1
  210.6 16.3 %fusion.13 = bf16[32,8,16,128]{3,1,2,0:T(8,128)(2,1)S(1)} fusion(bf16[8192,2048]{1,0:T(8,128)(2,1)} %all-gather.2.cloned.1.call-done, f32[8192]{0:T(1024)S(1)} %copy-done, f32[256]{0:T(256)S(1)} %add_rsqrt_fusion, bf16[256,8192]{1,0:T(8,128)(2,1)} %gather_fusion.1, pred[256]{0:T(512)(128)(4,1)S(1)} %compare_and_fusion.1, f32[2048]{0:T(1024)S(1)} %copy-done.1), kind=kOutput, calls=%fused_computation.15 | convolution fusion | flops 8601468928 | bytes 38839552 | tf_op jit(solution)/shard_map/dot_general | solution.py:73
  226.9 0.2 copy.14
  227.2 1.8 copy.12
  228.9 4.9 %all-to-all-start.1 = ((bf16[1,256,2,8,128]{4,2,1,0,3:T(2,128)(2,1)}), bf16[1,256,2,8,128]{4,2,1,0,3:T(2,128)(2,1)S(1)}, u32[]{:S(2)}, u32[]{:S(2)}) async-start(bf16[1,256,2,8,128]{4,2,1,0,3:T(2,128)(2,1)} %copy.12), calls=%async_computation.1 | async-start | bytes 2097152 | tf_op jit(solution)/shard_map/all_to_all | solution.py:81
  233.9 4.7 %bitcast_select_fusion = bf16[1,256,8192]{2,1,0:T(8,128)(2,1)} fusion(bf16[256,8192]{1,0:T(8,128)(2,1)} %gather_fusion.1, pred[256]{0:T(512)(128)(4,1)S(1)} %compare_and_fusion.1), kind=kLoop, calls=%fused_computation.9 | loop fusion | flops 2097152 | bytes 8388864 | tf_op jit(solution)/shard_map/jit(_take)/select_n | solution.py:54
  238.5 10.4 %all-to-all-done.1 = bf16[1,256,2,8,128]{4,2,1,0,3:T(2,128)(2,1)S(1)} async-done(((bf16[1,256,2,8,128]{4,2,1,0,3:T(2,128)(2,1)}), bf16[1,256,2,8,128]{4,2,1,0,3:T(2,128)(2,1)S(1)}, u32[]{:S(2)}, u32[]{:S(2)}) %all-to-all-start.1) | async-done | bytes 1048608 | tf_op jit(solution)/shard_map/all_to_all | solution.py:81
  249.0 1.0 copy.16
  (10 shorter events, 0.1 us)
Async XLA Ops:
  7.2 203.4 %all-gather.2.cloned.1.call-start = ((), (), s32[]{:S(2)}) async-start(), calls=%async_computation.2 | async-start | bytes 35651584 | tf_op jit(solution)/shard_map/all_gather | solution.py:75
  36.4 100.2 %all-to-all-start = ((bf16[8,64,8192]{2,1,0:T(8,128)(2,1)}), bf16[8,64,8192]{2,1,0:T(8,128)(2,1)}, u32[]{:S(2)}, u32[]{:S(2)}) async-start(bf16[8,64,8192]{2,1,0:T(8,128)(2,1)} %select_select_fusion), calls=%async_computation | async-start | bytes 16777216 | tf_op jit(solution)/shard_map/all_to_all | solution.py:68
  150.1 60.5 %copy-start = (f32[8192]{0:T(1024)S(1)}, f32[8192]{0:T(1024)}, u32[]{:S(2)}) copy-start(f32[8192]{0:T(1024)} %param.9) | copy-start | bytes 98308
  150.1 60.5 %copy-start.1 = (f32[2048]{0:T(1024)S(1)}, f32[2048]{0:T(1024)}, u32[]{:S(2)}) copy-start(f32[2048]{0:T(1024)} %param.11) | copy-start | bytes 24580
  228.9 20.0 %all-to-all-start.1 = ((bf16[1,256,2,8,128]{4,2,1,0,3:T(2,128)(2,1)}), bf16[1,256,2,8,128]{4,2,1,0,3:T(2,128)(2,1)S(1)}, u32[]{:S(2)}, u32[]{:S(2)}) async-start(bf16[1,256,2,8,128]{4,2,1,0,3:T(2,128)(2,1)} %copy.12), calls=%async_computation.1 | async-start | bytes 2097152 | tf_op jit(solution)/shard_map/all_to_all | solution.py:81
Sparse Core Ops, SparseCore 0:
  10.1 200.4 all-gather.1
where the time goes:
time: 257 us
  waiting for transfers between devices  162 us (63%)
  local copies, waits for them, and re-layouts  35.1 us (14%)
  other arithmetic  18.5 us (7%)
  matrix products  16.3 us (6%)
  between operations  14.1 us (5%)
  starting transfers between devices  11.3 us (4%)
    all_to_all x1, waiting for transfers between devices, on_device(): lax.all_to_all(outgoing, 'ctx', split_axis=0, concat_axis=0, tiled=True)  93.4 us
    all_gather x1, waiting for transfers between devices, on_device(): lax.all_gather(kv_weight, 'dp', axis=0, tiled=True)  57 us
    gather x1, local copies, waits for them, and re-layouts, pack_document_runs(): jnp.take(rows, wanted.reshape(-1), axis=0).reshape(peer_count, capacity, -1)  18.2 us
    dot_general x1, matrix products, on_device(): jnp.dot(normed, lax.all_gather(kv_weight, 'dp', axis=0, tiled=True), pref...  16.3 us
    gather x1, local copies, waits for them, and re-layouts, unpack_runs(): return jnp.take(flat_rows, source * capacity + within, axis=0)  13.6 us
    all_to_all x1, waiting for transfers between devices, on_device(): lax.all_to_all(mapped_outputs, 'ctx', split_axis=3, concat_axis=1, tiled=...  10.4 us
    select_n x1, other arithmetic, pack_document_runs(): return jnp.where(is_live[:, :, None], picked, jnp.zeros_like(picked))  7.59 us
    all_to_all x1, starting transfers between devices, on_device(): lax.all_to_all(outgoing, 'ctx', split_axis=0, concat_axis=0, tiled=True)  6.29 us
  transfers between devices with their start and end apart: 3, of which 3 were waited for; matrix products, arithmetic and copies ran while one was open for 20% of the time, Pallas kernels for 0%

commit v1 on v0

--- a/solution.py
+++ b/solution.py
@@ -2,9 +2,29 @@
 import jax.numpy as jnp
 from jax import lax
 from jax.sharding import PartitionSpec as P
+from jax.lax import axis_index, axis_size, ppermute
 
 KVH = 8
 HD = 128
+
+
+def push_the_ranges(t0):
+    axis_tag = "ctx"
+    built, carry_in = (axis_size(axis_tag), axis_index(axis_tag))
+    reached = t0.shape[3] // built
+    found_now = list(t0.shape)
+    found_now[3] = reached
+    v_next = found_now[1]
+    found_now[1] = v_next * built
+    s_next = jnp.zeros(found_now, t0.dtype)
+    for at in range(built):
+        w_next = lax.dynamic_slice_in_dim(t0, (carry_in ^ at) * reached, reached, axis=3)
+        if at:
+            w_next = ppermute(
+                w_next, axis_name=axis_tag, perm=[(j0, j0 ^ at) for j0 in range(built)]
+            )
+        s_next = lax.dynamic_update_slice_in_dim(s_next, w_next, (carry_in ^ at) * v_next, axis=1)
+    return s_next
 
 
 def plan_tables(lengths, targets, peer_count):
@@ -78,7 +98,7 @@
     mapped_outputs = (
         (summed_squares + kv_bias[None, :]).astype(jnp.bfloat16).reshape(1, row_count, 2, KVH, HD)
     )
-    by_heads = lax.all_to_all(mapped_outputs, "ctx", split_axis=3, concat_axis=1, tiled=True)
+    by_heads = push_the_ranges(mapped_outputs)
     return (moved_rows[None], by_heads)
 
 

time: 257 us -> 260 us (1.012)
  starting transfers between devices: 11.3 us -> 15.4 us
  waiting for transfers between devices: 162 us -> 159 us
  local copies, waits for them, and re-layouts: 35.1 us -> 37.7 us
    ppermute x0 -> x7, waiting for transfers between devices: none -> 11.1 us  [push_the_ranges(): ppermute(w_next, axis_name=axis_tag, perm=[(j0, j0 ^ at) for j0 in range(...]
    all_to_all x1 -> x0, waiting for transfers between devices: 10.4 us -> none  [on_device(): lax.all_to_all(mapped_outputs, 'ctx', split_axis=3, concat_axis=1, tiled=...]
    ppermute x0 -> x7, starting transfers between devices: none -> 9.09 us  [push_the_ranges(): ppermute(w_next, axis_name=axis_tag, perm=[(j0, j0 ^ at) for j0 in range(...]
    all_to_all x1 -> x0, starting transfers between devices: 4.93 us -> none  [on_device(): lax.all_to_all(mapped_outputs, 'ctx', split_axis=3, concat_axis=1, tiled=...]
  transfers between devices with their start and end apart: 3 -> 9, of which waited for: 3 -> 6; matrix products, arithmetic and copies ran while one was open for 20% -> 19% of each run, Pallas kernels for 0% -> 0%
where the time goes in v1:
time: 260 us
  waiting for transfers between devices  159 us (61%)
  local copies, waits for them, and re-layouts  37.7 us (15%)
  other arithmetic  16.5 us (6%)
  matrix products  16.4 us (6%)
  starting transfers between devices  15.4 us (6%)
  between operations  14.4 us (6%)
    all_to_all x1, waiting for transfers between devices, on_device(): lax.all_to_all(outgoing, 'ctx', split_axis=0, concat_axis=0, tiled=True)  93.3 us
    all_gather x1, waiting for transfers between devices, on_device(): lax.all_gather(kv_weight, 'dp', axis=0, tiled=True)  54.5 us
    gather x1, local copies, waits for them, and re-layouts, pack_document_runs(): jnp.take(rows, wanted.reshape(-1), axis=0).reshape(peer_count, capacity, -1)  18.2 us
    dot_general x1, matrix products, on_device(): jnp.dot(normed, lax.all_gather(kv_weight, 'dp', axis=0, tiled=True), pref...  16.4 us
    gather x1, local copies, waits for them, and re-layouts, unpack_runs(): return jnp.take(flat_rows, source * capacity + within, axis=0)  13.5 us
    ppermute x7, waiting for transfers between devices, push_the_ranges(): ppermute(w_next, axis_name=axis_tag, perm=[(j0, j0 ^ at) for j0 in range(...  11.1 us
    ppermute x7, starting transfers between devices, push_the_ranges(): ppermute(w_next, axis_name=axis_tag, perm=[(j0, j0 ^ at) for j0 in range(...  9.09 us
    select_n x1, other arithmetic, pack_document_runs(): return jnp.where(is_live[:, :, None], picked, jnp.zeros_like(picked))  7.59 us
  transfers between devices with their start and end apart: 9, of which 6 were waited for; matrix products, arithmetic and copies ran while one was open for 19% of the time, Pallas kernels for 0%

profile of v1, /device:TPU:1, one launch (start us, length us, event | category | flops | bytes accessed | tf_op | source)
XLA Modules:
  0.0 259.9 jit_solution(11941559758508850577)
XLA Ops:
  7.2 0.7 all-gather.2.cloned.1.call-update
  7.9 0.8 reduce_window_sum.23
  8.7 0.7 bitcast_subtract_fusion
  9.4 0.8 select_reduce_fusion.1
  10.4 18.2 %gather_fusion = bf16[512,8192]{1,0:T(8,128)(2,1)} fusion(bf16[256,8192]{1,0:T(8,128)(2,1)} %bitcast.21, s32[1024]{0:T(1024)S(1)} %pad_clamp_fusion.1), kind=kCustom, calls=%fused_computation | custom fusion | bytes 16779264 | tf_op jit(solution)/shard_map/jit(_take)/gather | solution.py:64
  28.8 7.6 %select_select_fusion = bf16[8,64,8192]{2,1,0:T(8,128)(2,1)} fusion(bf16[8,64,8192]{2,1,0:T(8,128)(2,1)} %bitcast.22, pred[8,64]{1,0:T(8,128)(4,1)S(1)} %compare_and_fusion, pred[8,64]{1,0:T(8,128)(4,1)S(1)} %iota_compare_fusion.3), kind=kLoop, calls=%fused_computation.7 | loop fusion | flops 8388608 | bytes 16778240 | tf_op jit(solution)/shard_map/jit(_where)/select_n | solution.py:65
  36.4 6.3 %all-to-all-start = ((bf16[8,64,8192]{2,1,0:T(8,128)(2,1)}), bf16[8,64,8192]{2,1,0:T(8,128)(2,1)}, u32[]{:S(2)}, u32[]{:S(2)}) async-start(bf16[8,64,8192]{2,1,0:T(8,128)(2,1)} %select_select_fusion), calls=%async_computation | async-start | bytes 16777216 | tf_op jit(solution)/shard_map/all_to_all | solution.py:88
  42.8 0.2 fusion.16
  43.3 93.3 %all-to-all-done = bf16[8,64,8192]{2,1,0:T(8,128)(2,1)} async-done(((bf16[8,64,8192]{2,1,0:T(8,128)(2,1)}), bf16[8,64,8192]{2,1,0:T(8,128)(2,1)}, u32[]{:S(2)}, u32[]{:S(2)}) %all-to-all-start) | async-done | bytes 8388640 | tf_op jit(solution)/shard_map/all_to_all | solution.py:88
  136.5 13.5 %gather_fusion.1 = bf16[256,8192]{1,0:T(8,128)(2,1)} fusion(bf16[512,8192]{1,0:T(8,128)(2,1)} %bitcast.7, s32[1024]{0:T(1024)S(1)} %pad_clamp_fusion), kind=kCustom, calls=%fused_computation.1 | custom fusion | bytes 8389632 | tf_op jit(solution)/shard_map/jit(_take)/gather | solution.py:74
  150.0 3.6 %fusion = f32[256]{0:T(256)S(1)} fusion(bf16[256,8192]{1,0:T(8,128)(2,1)} %gather_fusion.1, pred[256]{0:T(512)(128)(4,1)S(1)} %compare_and_fusion.1), kind=kLoop, calls=%fused_computation.4 | loop fusion | flops 8388352 | bytes 4195584 | tf_op jit(solution)/shard_map/reduce_sum | solution.py:52
  153.6 2.5 bitcast_select_fusion
  156.1 54.5 %all-gather.2.cloned.1.call-done = bf16[8192,2048]{1,0:T(8,128)(2,1)} async-done(((bf16[512,2048]{1,0:T(8,128)(2,1)}), bf16[8192,2048]{1,0:T(8,128)(2,1)}) %all-gather.2.cloned.1.call-update) | async-done | bytes 33554448 | tf_op jit(solution)/shard_map/all_gather | solution.py:95
  210.6 16.4 %fusion.13 = bf16[32,8,16,128]{3,1,2,0:T(8,128)(2,1)S(1)} fusion(bf16[8192,2048]{1,0:T(8,128)(2,1)} %all-gather.2.cloned.1.call-done, f32[8192]{0:T(1024)S(1)} %copy-done.2, f32[256]{0:T(256)S(1)} %add_rsqrt_fusion, bf16[256,8192]{1,0:T(8,128)(2,1)} %gather_fusion.1, pred[256]{0:T(512)(128)(4,1)S(1)} %compare_and_fusion.1, f32[2048]{0:T(1024)S(1)} %copy-done.3), kind=kOutput, calls=%fused_computation.15 | convolution fusion | flops 8601468928 | bytes 38839552 | tf_op jit(solution)/shard_map/dot_general | solution.py:93
  227.0 0.2 copy.40
  227.3 2.4 constant_dynamic-slice_fusion
  229.8 0.8 collective-permute-start
  230.7 1.3 collective-permute-start.1
  232.0 0.6 collective-permute-start.2
  232.7 2.8 %collective-permute-start.3 = (bf16[1,256,2,1,128]{4,2,3,1,0:T(2,128)(2,1)S(1)}, bf16[1,256,2,1,128]{4,2,3,1,0:T(2,128)(2,1)S(1)}, u32[]{:S(2)}, u32[]{:S(2)}) collective-permute-start(bf16[1,256,2,1,128]{4,2,3,1,0:T(2,128)(2,1)S(1)} %copy.36), channel_id=1, source_target_pairs={{0,4},{1,5},{2,6},{3,7},{4,0},{5,1},{6,2},{7,3},{8,12},{9,13},{10,... | collective-permute-start | bytes 393224 | tf_op jit(solution)/shard_map/ppermute | solution.py:23
  235.5 0.7 collective-permute-start.4
  236.3 0.6 broadcast_in_dim.56
  237.2 2.5 collective-permute-start.5
  239.6 0.1 constant_dynamic-update-slice_fusion.6
  239.8 0.5 collective-permute-start.6
  240.4 0.1 constant_dynamic-update-slice_fusion.4
  240.5 3.1 %collective-permute-done.3 = bf16[1,256,2,1,128]{4,2,3,1,0:T(2,128)(2,1)S(1)} collective-permute-done((bf16[1,256,2,1,128]{4,2,3,1,0:T(2,128)(2,1)S(1)}, bf16[1,256,2,1,128]{4,2,3,1,0:T(2,128)(2,1)S(1)}, u32[]{:S(2)}, u32[]{:S(2)}) %collective-permute-start.3) | collective-permute-done | bytes 131104 | tf_op jit(solution)/shard_map/ppermute | solution.py:23
  243.8 2.9 %collective-permute-done.4 = bf16[1,256,2,1,128]{4,2,3,1,0:T(2,128)(2,1)S(1)} collective-permute-done((bf16[1,256,2,1,128]{4,2,3,1,0:T(2,128)(2,1)S(1)}, bf16[1,256,2,1,128]{4,2,3,1,0:T(2,128)(2,1)S(1)}, u32[]{:S(2)}, u32[]{:S(2)}) %collective-permute-start.4) | collective-permute-done | bytes 131104 | tf_op jit(solution)/shard_map/ppermute | solution.py:23
  246.7 2.4 collective-permute-done.5
  249.3 2.7 %collective-permute-done.6 = bf16[1,256,2,1,128]{4,2,3,1,0:T(2,128)(2,1)S(1)} collective-permute-done((bf16[1,256,2,1,128]{4,2,3,1,0:T(2,128)(2,1)S(1)}, bf16[1,256,2,1,128]{4,2,3,1,0:T(2,128)(2,1)S(1)}, u32[]{:S(2)}, u32[]{:S(2)}) %collective-permute-start.6) | collective-permute-done | bytes 131104 | tf_op jit(solution)/shard_map/ppermute | solution.py:23
  251.9 0.1 constant_dynamic-update-slice_fusion
  252.1 1.0 copy-done.1
  (39 shorter events, 1.8 us)
Async XLA Ops:
  7.2 203.4 %all-gather.2.cloned.1.call-start = ((), (), s32[]{:S(2)}) async-start(), calls=%async_computation.1 | async-start | bytes 35651584 | tf_op jit(solution)/shard_map/all_gather | solution.py:95
  36.4 100.2 %all-to-all-start = ((bf16[8,64,8192]{2,1,0:T(8,128)(2,1)}), bf16[8,64,8192]{2,1,0:T(8,128)(2,1)}, u32[]{:S(2)}, u32[]{:S(2)}) async-start(bf16[8,64,8192]{2,1,0:T(8,128)(2,1)} %select_select_fusion), calls=%async_computation | async-start | bytes 16777216 | tf_op jit(solution)/shard_map/all_to_all | solution.py:88
  150.0 3.6 %copy-start = (bf16[256,8192]{1,0:T(8,128)(2,1)S(1)}, bf16[256,8192]{1,0:T(8,128)(2,1)}, u32[]{:S(2)}) copy-start(bf16[256,8192]{1,0:T(8,128)(2,1)} %gather_fusion.1) | copy-start | bytes 12582916
  153.6 57.0 %copy-start.2 = (f32[8192]{0:T(1024)S(1)}, f32[8192]{0:T(1024)}, u32[]{:S(2)}) copy-start(f32[8192]{0:T(1024)} %param.9) | copy-start | bytes 98308
  153.6 57.0 %copy-start.3 = (f32[2048]{0:T(1024)S(1)}, f32[2048]{0:T(1024)}, u32[]{:S(2)}) copy-start(f32[2048]{0:T(1024)} %param.11) | copy-start | bytes 24580
  229.8 7.3 %collective-permute-start = (bf16[1,256,2,1,128]{4,2,3,1,0:T(2,128)(2,1)S(1)}, bf16[1,256,2,1,128]{4,2,3,1,0:T(2,128)(2,1)S(1)}, u32[]{:S(2)}, u32[]{:S(2)}) collective-permute-start(bf16[1,256,2,1,128]{4,2,3,1,0:T(2,128)(2,1)S(1)} %copy.33), channel_id=1, source_target_pairs={{0,1},{1,0},{2,3},{3,2},{4,5},{5,4},{6,7},{7,6},{8,9},{9,8},{10,11... | collective-permute-start | bytes 393224 | tf_op jit(solution)/shard_map/ppermute | solution.py:23
  230.7 9.1 %collective-permute-start.1 = (bf16[1,256,2,1,128]{4,2,3,1,0:T(2,128)(2,1)S(1)}, bf16[1,256,2,1,128]{4,2,3,1,0:T(2,128)(2,1)S(1)}, u32[]{:S(2)}, u32[]{:S(2)}) collective-permute-start(bf16[1,256,2,1,128]{4,2,3,1,0:T(2,128)(2,1)S(1)} %copy.34), channel_id=1, source_target_pairs={{0,2},{1,3},{2,0},{3,1},{4,6},{5,7},{6,4},{7,5},{8,10},{9,11},{10,... | collective-permute-start | bytes 393224 | tf_op jit(solution)/shard_map/ppermute | solution.py:23
  232.0 8.4 %collective-permute-start.2 = (bf16[1,256,2,1,128]{4,2,3,1,0:T(2,128)(2,1)S(1)}, bf16[1,256,2,1,128]{4,2,3,1,0:T(2,128)(2,1)S(1)}, u32[]{:S(2)}, u32[]{:S(2)}) collective-permute-start(bf16[1,256,2,1,128]{4,2,3,1,0:T(2,128)(2,1)S(1)} %copy.35), channel_id=1, source_target_pairs={{0,3},{1,2},{2,1},{3,0},{4,7},{5,6},{6,5},{7,4},{8,11},{9,10},{10,... | collective-permute-start | bytes 393224 | tf_op jit(solution)/shard_map/ppermute | solution.py:23
  232.7 11.0 %collective-permute-start.3 = (bf16[1,256,2,1,128]{4,2,3,1,0:T(2,128)(2,1)S(1)}, bf16[1,256,2,1,128]{4,2,3,1,0:T(2,128)(2,1)S(1)}, u32[]{:S(2)}, u32[]{:S(2)}) collective-permute-start(bf16[1,256,2,1,128]{4,2,3,1,0:T(2,128)(2,1)S(1)} %copy.36), channel_id=1, source_target_pairs={{0,4},{1,5},{2,6},{3,7},{4,0},{5,1},{6,2},{7,3},{8,12},{9,13},{10,... | collective-permute-start | bytes 393224 | tf_op jit(solution)/shard_map/ppermute | solution.py:23
  235.5 11.1 %collective-permute-start.4 = (bf16[1,256,2,1,128]{4,2,3,1,0:T(2,128)(2,1)S(1)}, bf16[1,256,2,1,128]{4,2,3,1,0:T(2,128)(2,1)S(1)}, u32[]{:S(2)}, u32[]{:S(2)}) collective-permute-start(bf16[1,256,2,1,128]{4,2,3,1,0:T(2,128)(2,1)S(1)} %copy.37), channel_id=1, source_target_pairs={{0,5},{1,4},{2,7},{3,6},{4,1},{5,0},{6,3},{7,2},{8,13},{9,12},{10,... | collective-permute-start | bytes 393224 | tf_op jit(solution)/shard_map/ppermute | solution.py:23
  237.2 12.0 %collective-permute-start.5 = (bf16[1,256,2,1,128]{4,2,3,1,0:T(2,128)(2,1)S(1)}, bf16[1,256,2,1,128]{4,2,3,1,0:T(2,128)(2,1)S(1)}, u32[]{:S(2)}, u32[]{:S(2)}) collective-permute-start(bf16[1,256,2,1,128]{4,2,3,1,0:T(2,128)(2,1)S(1)} %copy.38), channel_id=1, source_target_pairs={{0,6},{1,7},{2,4},{3,5},{4,2},{5,3},{6,0},{7,1},{8,14},{9,15},{10,... | collective-permute-start | bytes 393224 | tf_op jit(solution)/shard_map/ppermute | solution.py:23
  239.8 12.2 %collective-permute-start.6 = (bf16[1,256,2,1,128]{4,2,3,1,0:T(2,128)(2,1)S(1)}, bf16[1,256,2,1,128]{4,2,3,1,0:T(2,128)(2,1)S(1)}, u32[]{:S(2)}, u32[]{:S(2)}) collective-permute-start(bf16[1,256,2,1,128]{4,2,3,1,0:T(2,128)(2,1)S(1)} %copy.39), channel_id=1, source_target_pairs={{0,7},{1,6},{2,5},{3,4},{4,3},{5,2},{6,1},{7,0},{8,15},{9,14},{10,... | collective-permute-start | bytes 393224 | tf_op jit(solution)/shard_map/ppermute | solution.py:23
  252.1 1.0 copy-start.1
Sparse Core Ops, SparseCore 0:
  10.1 200.4 all-gather.1
